TPU v7x, 32 devices: a whole 2x2x4 slice. The times are simulated.
32 devices in a mesh: feed: 8 (over z, x), tm: 4 (over y, core).
Axes of the slice: x: 2, y: 2, z: 4, core: 2. Of those that a mesh axis runs over, the one named last changes fastest.
Arguments:
- voltages: bfloat16 [2048, 131072], P('feed', 'tm'), may hold values from -6 to 6
- feed_slot: int32 [2048], replicated, may hold values from 0 to 2047, each once
- channel_flags: int32 [1024], replicated, may hold values from 0 to 1, as said below
Outputs:
- beam_power: float32 [96, 16, 1024], P(('feed', 'tm'))
Inputs may be any that keep to these rules, and one draw needn't show every extreme that they name: `channel_flags`: exactly 96 entries are 1. `feed_slot`: each slot is named by exactly one input.
All inputs are finite; a program needn't handle non-finite values.
Results may differ from a plain program's by a relative error of at most 0.01.
Values may be sent and summed in bfloat16 or wider, within the bound.
A program may use at most 128 MiB of HBM per device.

v0:
```python
import math

import jax
import jax.numpy as jnp
from jax import lax
from jax.sharding import PartitionSpec as P

CHANNELS = 1024
TAPS = 4
CYL = 4
NS = 256
UPCH = 16
LIVE_DEV = 3


def passed_along(block, axis, distance):
    devices = range(lax.axis_size(axis))
    route = [(i - distance, i) for i in devices if i - distance in devices]
    return lax.ppermute(block, axis, route)


def pfb_window():
    length = TAPS * 2 * CHANNELS
    sample = jnp.arange(length, dtype=jnp.float32)
    offset = (sample - length / 2 + 0.5) / (2 * CHANNELS)
    taper = 0.5 - 0.5 * jnp.cos(2.0 * jnp.pi * (sample + 0.5) / length)
    return (jnp.sinc(offset) * taper).reshape(TAPS, 2 * CHANNELS)


def phase_pair(modulus, first, second, scale):
    product = first[:, None] * second[None, :] % modulus
    angle = product.astype(jnp.float32) * (2.0 * jnp.pi / modulus)
    return (jnp.cos(angle) * scale, jnp.sin(angle) * scale)


def grid_table():
    index = jnp.arange(NS, dtype=jnp.int32)
    cosine, sine = phase_pair(NS, index, index, 1.0 / math.sqrt(NS))
    cosine = cosine.astype(jnp.bfloat16)
    sine = sine.astype(jnp.bfloat16)
    return cosine, sine


def live_channels(flags, count):
    k = jnp.arange(flags.shape[0], dtype=jnp.int32)
    seen = jnp.sum(jnp.where(k[None, :] <= k[:, None], flags[None, :], 0), axis=1)
    j = jnp.arange(count, dtype=jnp.int32)
    return jnp.sum((seen[None, :] <= j[:, None]).astype(jnp.int32), axis=1)


def pfb_filter(voltages, n_frames, window):
    inputs = voltages.shape[0]
    frames = voltages.reshape(inputs, n_frames, 2 * CHANNELS).astype(jnp.float32)
    padded = jnp.pad(frames, ((0, 0), (TAPS - 1, TAPS - 1), (0, 0)))
    total = n_frames + TAPS - 1
    summed = 0.0
    for tap in range(TAPS):
        summed = summed + window[tap] * padded[:, tap : tap + total]
    return summed.astype(jnp.bfloat16)


def local(voltages, feed_slot, channel_flags):
    n_frames = voltages.shape[1] // (2 * CHANNELS)
    n_time = lax.axis_size("tm")
    n_feed = lax.axis_size("feed")
    inputs = voltages.shape[0]
    live_count = LIVE_DEV * n_feed * n_time
    chans = LIVE_DEV * n_time
    live = live_channels(channel_flags, live_count)
    cosine, sine = phase_pair(
        2 * CHANNELS, live, jnp.arange(2 * CHANNELS, dtype=jnp.int32), 1.0 / math.sqrt(2 * CHANNELS)
    )
    coeffs = jnp.stack([cosine, -sine]).astype(jnp.bfloat16)
    filtered = pfb_filter(voltages, n_frames, pfb_window())
    spectra = jnp.einsum("rcs,ifs->rcfi", coeffs, filtered, preferred_element_type=jnp.float32)
    earlier = passed_along(spectra[:, :, n_frames:].astype(jnp.bfloat16), "tm", 1)
    spectra = spectra[:, :, :n_frames]
    spectra = jnp.concatenate(
        [spectra[:, :, : TAPS - 1] + earlier.astype(jnp.float32), spectra[:, :, TAPS - 1 :]], axis=2
    ).astype(jnp.bfloat16)
    turned = lax.all_to_all(
        spectra.reshape(2, n_feed, chans, n_frames, inputs), "feed", split_axis=1, concat_axis=1, tiled=True
    )
    slots = feed_slot.reshape(n_feed, inputs)
    onehot = (slots[:, :, None] == jnp.arange(n_feed * inputs, dtype=jnp.int32)).astype(jnp.bfloat16)
    cells = jnp.einsum(
        "rscfi,sin->rcfn", turned, onehot, preferred_element_type=jnp.float32
    ).astype(jnp.bfloat16)
    cells = cells.reshape(2, chans, n_frames, 2 * CYL, NS)
    cosine, sine = grid_table()
    table = jnp.stack([jnp.stack([cosine, -sine], axis=1), jnp.stack([sine, cosine], axis=1)])
    ns_out = jnp.einsum("rcfgm,rmqn->qcfgn", cells, table, preferred_element_type=jnp.float32)
    z = ns_out.reshape(2, chans, n_frames, 2, CYL, NS)
    re, im = z[0], z[1]
    r = [re[:, :, :, y] for y in range(CYL)]
    i = [im[:, :, :, y] for y in range(CYL)]
    t0r, t1r, t2r, t3r = r[0] + r[2], r[0] - r[2], r[1] + r[3], r[1] - r[3]
    t0i, t1i, t2i, t3i = i[0] + i[2], i[0] - i[2], i[1] + i[3], i[1] - i[3]
    beam_re = jnp.stack([t0r + t2r, t1r + t3i, t0r - t2r, t1r - t3i], axis=3)
    beam_im = jnp.stack([t0i + t2i, t1i - t3r, t0i - t2i, t1i + t3r], axis=3)
    beams = (jnp.stack([beam_re, beam_im]) * 0.5).astype(jnp.bfloat16)
    blocks = n_frames // UPCH
    beams = beams.reshape(2, chans, blocks, UPCH, 2, CYL * NS)
    index = jnp.arange(UPCH, dtype=jnp.int32)
    up_cos, up_sin = phase_pair(UPCH, index, index, 1.0 / math.sqrt(UPCH))
    up_cos = up_cos.astype(jnp.bfloat16)
    up_sin = up_sin.astype(jnp.bfloat16)
    up_table = jnp.stack([jnp.stack([up_cos, -up_sin], axis=1), jnp.stack([up_sin, up_cos], axis=1)])
    up = jnp.einsum("qcbupn,quvk->vcbkpn", beams, up_table, preferred_element_type=jnp.float32)
    power = jnp.sum(up * up, axis=(0, 2, 4)) * (1.0 / (2.0 * n_time * blocks))
    parts = lax.all_to_all(
        power.astype(jnp.bfloat16).reshape(n_time, LIVE_DEV, UPCH, CYL * NS), "tm", split_axis=0, concat_axis=0, tiled=True
    )
    return jnp.sum(parts.astype(jnp.float32), axis=0)


def solution(mesh):
    in_specs = (P("feed", "tm"), P(), P())
    out_specs = P(("feed", "tm"), None, None)
    return jax.shard_map(local, mesh=mesh, in_specs=in_specs, out_specs=out_specs, check_vma=False)
```

profile of v0, /device:TPU:0, one launch (start us, length us, event | category | flops | bytes accessed | tf_op | source)
XLA Modules:
  0.0 155.9 jit_solution(15746249527885621459)
XLA Ops:
  0.0 0.2 fusion.50
  0.2 0.9 select_reduce_fusion
  1.1 0.1 convert_reduce_fusion.1
  1.2 3.7 %multiply_convert_fusion.1 = (bf16[1,96,2048]{2,1,0:T(8,128)(2,1)S(1)}, bf16[1,96,2048]{2,1,0:T(8,128)(2,1)S(1)}) fusion(s32[96]{0:T(128)S(1)} %convert_reduce_fusion.1), kind=kLoop, calls=%fused_computation.44 | loop fusion | flops 3735552 | bytes 786816 | tf_op jit(solution)/shard_map/convert.9
  4.9 8.1 %copy.58 = bf16[32,16,8,2048]{3,2,0,1:T(8,128)(2,1)S(1)} copy(bf16[32,16,8,2048]{3,2,1,0:T(8,128)(2,1)} %bitcast.89) | data formatting | bytes 33554432 | tf_op jit(solution)/shard_map/convert_element_type | solution.py:53
  13.0 15.4 %pad_convert_fusion = f32[256,22,2048]{2,0,1:T(8,128)} fusion(bf16[256,16,2048]{2,0,1:T(8,128)(2,1)S(1)} %bitcast.88), kind=kLoop, calls=%fused_computation.8 | loop fusion | flops 11534336 | bytes 62914560 | tf_op jit(solution)/shard_map/jit(_pad)/pad | solution.py:54
  28.3 49.6 %fusion.91 = (bf16[2,96,19,256]{3,1,0,2:T(8,128)(2,1)S(1)}, f32[2,96,19,256]{3,1,0,2:T(8,128)S(1)}) fusion(bf16[1,96,2048]{2,1,0:T(8,128)(2,1)S(1)} %get-tuple-element.24, bf16[1,96,2048]{2,1,0:T(8,128)(2,1)S(1)} %get-tuple-element.23, f32[256,22,2048]{2,0,1:T(8,128)} %pad_convert_fusion, f32[2048]{0:T(1024)S(1)} %get-tuple-element.18, ...), kind=kOutput, calls=%fused_computation.146 | convolution fusion | flops 3907403776 | bytes 165806080 | tf_op jit(solution)/shard_map/rcs,ifs->rcfi/dot_general | solution.py:75
  78.0 2.4 %collective-permute-start = (bf16[2,96,3,256]{3,1,0,2:T(8,128)(2,1)S(1)}, bf16[2,96,3,256]{3,1,0,2:T(8,128)(2,1)S(1)}, u32[]{:S(2)}, u32[]{:S(2)}) collective-permute-start(bf16[2,96,3,256]{3,1,0,2:T(8,128)(2,1)S(1)} %slice.104), channel_id=1, source_target_pairs={{0,1},{1,2},{2,3},{4,5},{5,6},{6,7},{8,9},{9,10},{10,11},{12,13},{... | collective-permute-start | bytes 884744 | tf_op jit(solution)/shard_map/ppermute | solution.py:19
  80.4 0.1 slice.105
  80.5 1.3 copy.36
  81.8 0.0 collective-permute-done
  81.8 0.1 fusion.28
  81.9 0.3 copy.35
  82.2 2.0 %pad_maximum_fusion = bf16[2,8,12,16,256]{4,0,3,2,1:T(2,128)(2,1)S(1)} fusion(bf16[2,8,12,13,256]{4,0,3,2,1:T(2,128)(2,1)S(1)} %bitcast.94, bf16[2,8,12,3,256]{4,0,3,2,1:T(2,128)(2,1)S(1)} %bitcast.97), kind=kLoop, calls=%fused_computation.28 | loop fusion | flops 786432 | bytes 3145728 | tf_op jit(solution)/shard_map/concatenate | solution.py:78
  84.2 1.5 copy.37
  85.7 0.0 copy-start.1
  85.7 6.8 %all-to-all-start = ((bf16[2,8,12,16,256]{4,3,2,0,1:T(8,128)(2,1)}), bf16[2,8,12,16,256]{4,3,2,0,1:T(8,128)(2,1)S(1)}, u32[]{:S(2)}, u32[]{:S(2)}) async-start(bf16[2,8,12,16,256]{4,3,2,0,1:T(8,128)(2,1)} %copy.37), calls=%async_computation | async-start | bytes 3145728 | tf_op jit(solution)/shard_map/all_to_all | solution.py:81
  92.5 0.0 copy-done.1
  92.5 0.1 fusion.83
  92.6 0.1 multiply_convert_fusion.4
  92.6 1.0 fusion.45
  93.6 1.3 multiply_convert_fusion.2
  95.0 34.3 %all-to-all-done = bf16[2,8,12,16,256]{4,3,2,0,1:T(8,128)(2,1)S(1)} async-done(((bf16[2,8,12,16,256]{4,3,2,0,1:T(8,128)(2,1)}), bf16[2,8,12,16,256]{4,3,2,0,1:T(8,128)(2,1)S(1)}, u32[]{:S(2)}, u32[]{:S(2)}) %all-to-all-start) | async-done | bytes 1572896 | tf_op jit(solution)/shard_map/all_to_all | solution.py:81
  129.3 3.8 %fusion.8 = bf16[2,12,16,2048,1]{3,2,1,0,4:T(8,128)(2,1)S(1)} fusion(bf16[2,8,12,16,256]{4,3,2,0,1:T(8,128)(2,1)S(1)} %all-to-all-done, s32[8,256]{1,0:T(8,128)S(1)} %eq.59), kind=kOutput, calls=%fused_computation.14 | convolution fusion | flops 3225419776 | bytes 3153920 | tf_op jit(solution)/shard_map/rscfi,sin->rcfn/dot_general | solution.py:86
  133.1 0.1 copy.59
  133.2 1.0 convolution_bitcast_fusion
  134.2 0.5 fusion.89
  134.7 0.2 fusion.44
  134.8 0.4 fusion.40
  135.2 0.2 fusion.38
  135.3 0.2 pad_maximum_fusion.2
  135.5 1.2 copy.41
  136.8 2.0 %stack.81 = f32[1,12,16,2,1024]{4,2,0,3,1:T(8,128)} reshape(f32[12,16,2,4,256]{4,3,1,2,0:T(4,128)S(1)} %copy.41) | data formatting | bytes 3145728 | tf_op jit(solution)/shard_map/stack | solution.py:101
  138.8 0.1 pad_maximum_fusion.1
  138.9 1.2 copy.40
  140.1 0.0 copy-start
  140.1 2.0 %stack.79 = f32[1,12,16,2,1024]{4,2,0,3,1:T(8,128)} reshape(f32[12,16,2,4,256]{4,3,1,2,0:T(4,128)S(1)} %copy.40) | data formatting | bytes 3145728 | tf_op jit(solution)/shard_map/stack | solution.py:101
  142.1 0.0 copy-done
  142.1 2.1 %fusion.12 = f32[16,12,1024]{2,0,1:T(8,128)S(1)} fusion(f32[1,12,16,2,1024]{4,2,0,3,1:T(8,128)S(1)} %copy-done, f32[1,12,16,2,1024]{4,2,0,3,1:T(8,128)} %stack.79, bf16[1,16,2,16]{1,3,0,2:T(8,128)(2,1)S(1)} %get-tuple-element.22, bf16[1,16,2,16]{1,3,0,2:T(8,128)(2,1)S(1)} %get-tuple-element.21), kind=kOutput, calls=%fused_computation.21 | convolution fusion | flops 54071296 | bytes 3934208 | tf_op jit(solution)/shard_map/qcbupn,quvk->vcbkpn/dot_general | solution.py:109
  144.2 0.1 multiply_convert_fusion
  144.3 10.9 %all_to_all.10 = bf16[4,3,16,1024]{3,2,1,0:T(8,128)(2,1)S(1)} all-to-all(bf16[4,3,16,1024]{3,2,1,0:T(8,128)(2,1)S(1)} %bitcast.96), channel_id=1, replica_groups=mesh['feed'=8,'tm'=4] {'tm'}, dimensions={0} | all-to-all | bytes 786432 | tf_op jit(solution)/shard_map/all_to_all | solution.py:111
  155.2 0.7 convert_reduce_fusion
  (5 shorter events, 0.1 us)
Async XLA Ops:
  78.0 3.8 %collective-permute-start = (bf16[2,96,3,256]{3,1,0,2:T(8,128)(2,1)S(1)}, bf16[2,96,3,256]{3,1,0,2:T(8,128)(2,1)S(1)}, u32[]{:S(2)}, u32[]{:S(2)}) collective-permute-start(bf16[2,96,3,256]{3,1,0,2:T(8,128)(2,1)S(1)} %slice.104), channel_id=1, source_target_pairs={{0,1},{1,2},{2,3},{4,5},{5,6},{6,7},{8,9},{9,10},{10,11},{12,13},{... | collective-permute-start | bytes 884744 | tf_op jit(solution)/shard_map/ppermute | solution.py:19
  85.7 6.8 %copy-start.1 = (s32[2048]{0:T(1024)S(1)}, s32[2048]{0:T(1024)}, u32[]{:S(2)}) copy-start(s32[2048]{0:T(1024)} %param.4) | copy-start | bytes 24580
  85.7 43.5 %all-to-all-start = ((bf16[2,8,12,16,256]{4,3,2,0,1:T(8,128)(2,1)}), bf16[2,8,12,16,256]{4,3,2,0,1:T(8,128)(2,1)S(1)}, u32[]{:S(2)}, u32[]{:S(2)}) async-start(bf16[2,8,12,16,256]{4,3,2,0,1:T(8,128)(2,1)} %copy.37), calls=%async_computation | async-start | bytes 3145728 | tf_op jit(solution)/shard_map/all_to_all | solution.py:81
  140.1 2.0 %copy-start = (f32[1,12,16,2,1024]{4,2,0,3,1:T(8,128)S(1)}, f32[1,12,16,2,1024]{4,2,0,3,1:T(8,128)}, u32[]{:S(2)}) copy-start(f32[1,12,16,2,1024]{4,2,0,3,1:T(8,128)} %stack.81) | copy-start | bytes 4718596
where the time goes:
time: 156 us
  matrix products  56.5 us (36%)
  waiting for transfers between devices  34.3 us (22%)
  other arithmetic  26.6 us (17%)
  local copies, waits for them, and re-layouts  18.3 us (12%)
  blocking collectives  10.9 us (7%)
  starting transfers between devices  9.17 us (6%)
    dot_general x1, matrix products, local(): jnp.einsum('rcs,ifs->rcfi', coeffs, filtered, preferred_element_type=jnp....  49.6 us
    all_to_all x1, waiting for transfers between devices, local(): lax.all_to_all(spectra.reshape(2, n_feed, chans, n_frames, inputs), 'feed...  34.3 us
    pad x1, other arithmetic, pfb_filter(): padded = jnp.pad(frames, ((0, 0), (TAPS - 1, TAPS - 1), (0, 0)))  15.4 us
    all_to_all x1, blocking collectives, local(): lax.all_to_all(power.astype(jnp.bfloat16).reshape(n_time, LIVE_DEV, UPCH,...  10.9 us
    convert_element_type x1, local copies, waits for them, and re-layouts, pfb_filter(): voltages.reshape(inputs, n_frames, 2 * CHANNELS).astype(jnp.float32)  8.06 us
    all_to_all x1, starting transfers between devices, local(): lax.all_to_all(spectra.reshape(2, n_feed, chans, n_frames, inputs), 'feed...  6.75 us
    another operation x2, local copies, waits for them, and re-layouts, local(): beams = (jnp.stack([beam_re, beam_im]) * 0.5).astype(jnp.bfloat16)  3.94 us
    dot_general x1, matrix products, local(): jnp.einsum('rscfi,sin->rcfn', turned, onehot, preferred_element_type=jnp....  3.8 us
  transfers between devices with their start and end apart: 2, of which 1 were waited for; matrix products, arithmetic and copies ran while one was open for 2% of the time, Pallas kernels for 0%

commit v1 on v0

--- a/solution.py
+++ b/solution.py
@@ -1,8 +1,12 @@
 import math
+
+import functools
 
 import jax
 import jax.numpy as jnp
 from jax import lax
+from jax.experimental import pallas as pl
+from jax.experimental.pallas import tpu as pltpu
 from jax.sharding import PartitionSpec as P
 
 CHANNELS = 1024
@@ -59,7 +63,7 @@
     return summed.astype(jnp.bfloat16)
 
 
-def local(voltages, feed_slot, channel_flags):
+def local_plain(voltages, feed_slot, channel_flags):
     n_frames = voltages.shape[1] // (2 * CHANNELS)
     n_time = lax.axis_size("tm")
     n_feed = lax.axis_size("feed")
@@ -114,6 +118,337 @@
     return jnp.sum(parts.astype(jnp.float32), axis=0)
 
 
+MESH = pl.DeviceIdType.MESH
+NT = (((1,), (1,)), ((), ()))
+
+
+def fused_kernel(
+    n_feed, n_time, n_frames, scale,
+    volt, coeffs, window, slots, t1, t2, upm, out,
+    vp, filt, tmp, send, recv, hist_out, hist_in, onehot, acc, cells, beams, power, psend, precv,
+    load_sem, own_sem, hist_sem, send_sem, recv_sem, psend_sem, precv_sem,
+):
+    me = lax.axis_index("feed")
+    tm = lax.axis_index("tm")
+    frame = 2 * CHANNELS
+    past = TAPS - 1
+    quads = n_frames // 4
+    inputs = volt.shape[0]
+    rows = coeffs.shape[0]
+    own_rows = LIVE_DEV * UPCH
+
+    def load(f):
+        return pltpu.make_async_copy(
+            volt.at[:, f * frame : (f + 1) * frame], vp.at[f + past], load_sem.at[f]
+        )
+
+    order = list(range(n_frames - past, n_frames)) + list(range(1, n_frames - past)) + [0]
+    for f in order:
+        load(f).start()
+    barrier = pltpu.get_barrier_semaphore()
+    for o in range(1, n_feed):
+        pl.semaphore_signal(barrier, inc=1, device_id={"feed": lax.rem(me + o, n_feed)}, device_id_type=MESH)
+    for o in range(1, n_time):
+        pl.semaphore_signal(barrier, inc=1, device_id={"tm": lax.rem(tm + o, n_time)}, device_id_type=MESH)
+    pl.semaphore_wait(barrier, n_feed - 1 + n_time - 1)
+
+    for t in range(past):
+        vp[t] = jnp.zeros_like(vp[t])
+        vp[n_frames + past + t] = jnp.zeros_like(vp[t])
+
+    def spectra(f):
+        width = 256
+
+        def chunk(c, _):
+            lanes = pl.ds(pl.multiple_of(c * width, width), width)
+            total = window[0:1, lanes] * vp[f, :, lanes].astype(jnp.float32)
+            for t in range(1, TAPS):
+                total = total + window[t : t + 1, lanes] * vp[f + t, :, lanes].astype(jnp.float32)
+            filt[:, lanes] = total.astype(jnp.bfloat16)
+            return 0
+
+        lax.fori_loop(0, frame // width, chunk, 0)
+        return lax.dot_general(coeffs[...], filt[...], NT, preferred_element_type=jnp.float32)
+
+    for f in range(n_frames - past, n_frames):
+        load(f).wait()
+
+    def tail_frame(k, _):
+        hist_out[k] = spectra(n_frames + k).astype(jnp.bfloat16)
+        return 0
+
+    lax.fori_loop(0, past, tail_frame, 0)
+
+    def hist_copy(to):
+        return pltpu.make_async_remote_copy(
+            src_ref=hist_out, dst_ref=hist_in, send_sem=hist_sem.at[0], recv_sem=hist_sem.at[1],
+            device_id={"tm": to}, device_id_type=MESH,
+        )
+
+    @pl.when(tm < n_time - 1)
+    def _():
+        hist_copy(lax.rem(tm + 1, n_time)).start()
+
+    def send_copy(q, o):
+        to = lax.rem(me + o, n_feed)
+        return pltpu.make_async_remote_copy(
+            src_ref=send.at[q, to], dst_ref=recv.at[me, :, q],
+            send_sem=send_sem.at[q, o], recv_sem=recv_sem.at[q, o],
+            device_id={"feed": to}, device_id_type=MESH,
+        )
+
+    def arrival(q, o):
+        back = lax.rem(me + n_feed - o, n_feed)
+        return pltpu.make_async_remote_copy(
+            src_ref=send.at[q, back], dst_ref=recv.at[back, :, q],
+            send_sem=send_sem.at[q, o], recv_sem=recv_sem.at[q, o],
+            device_id={"feed": back}, device_id_type=MESH,
+        )
+
+    def own_copy(q):
+        return pltpu.make_async_copy(send.at[q, me], recv.at[me, :, q], own_sem.at[q])
+
+    def far_first(k):
+        return lax.rem(k + n_feed // 2 - 1, n_feed - 1) + 1
+
+    lower = lax.broadcasted_iota(jnp.int32, (8, inputs), 0) < 4
+
+    def quad(q, first):
+        def one(k, _):
+            value = spectra(q * 4 + k)
+            if first:
+                value = value + jnp.where(k < past, 1.0, 0.0) * hist_in[jnp.minimum(k, past - 1)].astype(jnp.float32)
+            tmp[k] = value
+            return 0
+
+        lax.fori_loop(0, 4, one, 0)
+
+        def pack(d, _):
+            parts = [[], []]
+            at = pl.multiple_of(d * 24, 8)
+            for pair in range(2):
+                a0, b0, c0 = (tmp[2 * pair, pl.ds(at + 8 * k, 8)] for k in range(3))
+                a1, b1, c1 = (tmp[2 * pair + 1, pl.ds(at + 8 * k, 8)] for k in range(3))
+                parts[0] += [a0, a1, jnp.where(lower, b0, pltpu.roll(b1, 4, 0))]
+                parts[1] += [c0, c1, jnp.where(lower, pltpu.roll(b0, 4, 0), b1)]
+            send[q, d, 0] = jnp.concatenate(parts[0], axis=0).astype(jnp.bfloat16)
+            send[q, d, 1] = jnp.concatenate(parts[1], axis=0).astype(jnp.bfloat16)
+            return 0
+
+        lax.fori_loop(0, n_feed, pack, 0)
+
+        def start(k, _):
+            send_copy(q, far_first(k)).start()
+            return 0
+
+        lax.fori_loop(0, n_feed - 1, start, 0)
+        own_copy(q).start()
+
+    for f in range(1, 4):
+        load(f).wait()
+    for q in range(1, quads):
+        for f in range(4 * q, min(4 * q + 4, n_frames - past)):
+            load(f).wait()
+        quad(q, False)
+    load(0).wait()
+
+    @pl.when(tm > 0)
+    def _():
+        hist_copy(lax.rem(tm + n_time - 1, n_time)).wait_recv()
+
+    @pl.when(tm == 0)
+    def _():
+        hist_in[...] = jnp.zeros_like(hist_in)
+
+    quad(0, True)
+
+    total = n_feed * inputs
+    which = lax.broadcasted_iota(jnp.int32, (total, inputs), 0)
+
+    def ones(s, _):
+        onehot[s] = jnp.where(which == slots[s], 1.0, 0.0).astype(jnp.bfloat16)
+        return 0
+
+    lax.fori_loop(0, n_feed, ones, 0)
+
+    step = 512
+
+    def place(s, fresh):
+        block = recv[s].reshape(2 * quads * 48, inputs)
+
+        def part(n, _):
+            at = pl.multiple_of(n * step, step)
+            got = lax.dot_general(block, onehot[s, pl.ds(at, step), :], NT, preferred_element_type=jnp.float32)
+            if fresh:
+                acc[:, pl.ds(at, step)] = got
+            else:
+                acc[:, pl.ds(at, step)] += got
+            return 0
+
+        lax.fori_loop(0, total // step, part, 0)
+
+    for q in range(quads):
+        own_copy(q).wait()
+    place(me, True)
+
+    def source(k, _):
+        o = lax.rem(k, n_feed - 1) + 1
+        for q in range(quads):
+            arrival(q, o).wait_recv()
+        place(lax.rem(me + n_feed - o, n_feed), False)
+        return 0
+
+    lax.fori_loop(0, n_feed - 1, source, 0)
+    half = quads * 48
+    cells[...] = acc[...].astype(jnp.bfloat16)
+
+    for p in range(2):
+        z = []
+        for y in range(CYL):
+            at = (p * CYL + y) * NS
+            value = jnp.dot(cells[:half, at : at + NS], t1[...], preferred_element_type=jnp.float32)
+            value = value + jnp.dot(cells[half:, at : at + NS], t2[...], preferred_element_type=jnp.float32)
+            z.append((value[:, :NS], value[:, NS:]))
+        (r0, i0), (r1, i1), (r2, i2), (r3, i3) = z
+        t0r, t1r, t2r, t3r = r0 + r2, r0 - r2, r1 + r3, r1 - r3
+        t0i, t1i, t2i, t3i = i0 + i2, i0 - i2, i1 + i3, i1 - i3
+        re = [t0r + t2r, t1r + t3i, t0r - t2r, t1r - t3i]
+        im = [t0i + t2i, t1i - t3r, t0i - t2i, t1i + t3r]
+        for e in range(CYL):
+            at = (p * CYL + e) * NS
+            beams[:half, at : at + NS] = (re[e] * 0.5).astype(jnp.bfloat16)
+            beams[half:, at : at + NS] = (im[e] * 0.5).astype(jnp.bfloat16)
+
+    outs = upm.shape[0] // 2
+    for e in range(CYL):
+        summed = 0.0
+        for p in range(2):
+            at = (p * CYL + e) * NS
+            up = jnp.dot(upm[...], beams[:, at : at + NS], preferred_element_type=jnp.float32)
+            summed = summed + up[:outs] * up[:outs] + up[outs:] * up[outs:]
+        summed = summed * scale
+        for t in range(n_time):
+            block = summed[t * own_rows : (t + 1) * own_rows]
+            power[t, :, e * NS : (e + 1) * NS] = block
+            psend[t, :, e * NS : (e + 1) * NS] = block.astype(jnp.bfloat16)
+
+    def power_copy(o):
+        to = lax.rem(tm + o, n_time)
+        return pltpu.make_async_remote_copy(
+            src_ref=psend.at[to], dst_ref=precv.at[o - 1],
+            send_sem=psend_sem.at[o - 1], recv_sem=precv_sem.at[o - 1],
+            device_id={"tm": to}, device_id_type=MESH,
+        )
+
+    for o in range(1, n_time):
+        power_copy(o).start()
+    result = power[tm]
+    for o in range(1, n_time):
+        power_copy(o).wait_recv()
+        result = result + precv[o - 1].astype(jnp.float32)
+    out[...] = result
+    for o in range(1, n_time):
+        power_copy(o).wait_send()
+
+    def drain(k, _):
+        for q in range(quads):
+            send_copy(q, k + 1).wait_send()
+        return 0
+
+    lax.fori_loop(0, n_feed - 1, drain, 0)
+
+    @pl.when(tm < n_time - 1)
+    def _():
+        hist_copy(lax.rem(tm + 1, n_time)).wait_send()
+
+
+def row_order(quads):
+    frames, chans = [], []
+    for q in range(quads):
+        for pair in range(2):
+            f = 4 * q + 2 * pair
+            frames += [f] * 8 + [f + 1] * 8 + [f] * 4 + [f + 1] * 4
+            chans += list(range(8)) * 2 + list(range(8, 12)) * 2
+    return jnp.array(frames, jnp.int32), jnp.array(chans, jnp.int32)
+
+
+def local_fused(voltages, feed_slot, channel_flags):
+    bf16 = jnp.bfloat16
+    frame = 2 * CHANNELS
+    inputs = voltages.shape[0]
+    n_frames = voltages.shape[1] // frame
+    n_time = lax.axis_size("tm")
+    n_feed = lax.axis_size("feed")
+    chans = LIVE_DEV * n_time
+    quads = n_frames // 4
+    live = live_channels(channel_flags, chans * n_feed).reshape(n_feed, chans)
+    row_chan = jnp.concatenate([live, live[:, 8:], live[:, :8]], axis=1).reshape(-1)
+    is_imag = jnp.tile(jnp.arange(2 * chans) >= chans, n_feed)
+    product = row_chan[:, None] * jnp.arange(frame, dtype=jnp.int32)[None, :] % frame
+    angle = product.astype(jnp.float32) * (2.0 * jnp.pi / frame)
+    coeffs = jnp.where(is_imag[:, None], -jnp.sin(angle), jnp.cos(angle)) * (1.0 / math.sqrt(frame))
+    coeffs = coeffs.astype(bf16)
+    c, d = grid_table()
+    t1 = jnp.concatenate([c, -d], axis=1)
+    t2 = jnp.concatenate([d, c], axis=1)
+    index = jnp.arange(UPCH, dtype=jnp.int32)
+    frames, row_ch = row_order(quads)
+    up_cos, up_sin = phase_pair(UPCH, index, frames, 1.0 / math.sqrt(UPCH))
+    same = (jnp.arange(chans)[:, None] == row_ch[None, :])[:, None, :]
+    cm = jnp.where(same, up_cos[None], 0.0).reshape(chans * UPCH, -1)
+    sm = jnp.where(same, up_sin[None], 0.0).reshape(chans * UPCH, -1)
+    upm = jnp.concatenate([jnp.concatenate([cm, sm], 1), jnp.concatenate([-sm, cm], 1)], 0).astype(bf16)
+    rows = 2 * chans * n_feed
+    total = n_feed * inputs
+    own_rows = LIVE_DEV * UPCH
+    half = quads * 48
+    vmem = pl.BlockSpec(memory_space=pltpu.VMEM)
+    dma = pltpu.SemaphoreType.DMA
+    result = pl.pallas_call(
+        functools.partial(fused_kernel, n_feed, n_time, n_frames, 1.0 / (2.0 * n_time)),
+        out_shape=jax.ShapeDtypeStruct((own_rows, CYL * NS), jnp.float32),
+        in_specs=[pl.BlockSpec(memory_space=pl.ANY)] + [vmem] * 6,
+        out_specs=vmem,
+        scratch_shapes=[
+            pltpu.VMEM((n_frames + 2 * TAPS - 2, inputs, frame), bf16),
+            pltpu.VMEM((inputs, frame), bf16),
+            pltpu.VMEM((4, rows, inputs), jnp.float32),
+            pltpu.VMEM((quads, n_feed, 2, 48, inputs), bf16),
+            pltpu.VMEM((n_feed, 2, quads, 48, inputs), bf16),
+            pltpu.VMEM((TAPS - 1, rows, inputs), bf16),
+            pltpu.VMEM((TAPS - 1, rows, inputs), bf16),
+            pltpu.VMEM((n_feed, total, inputs), bf16),
+            pltpu.VMEM((2 * half, total), jnp.float32),
+            pltpu.VMEM((2 * half, total), bf16),
+            pltpu.VMEM((2 * half, total), bf16),
+            pltpu.VMEM((n_time, own_rows, CYL * NS), jnp.float32),
+            pltpu.VMEM((n_time, own_rows, CYL * NS), bf16),
+            pltpu.VMEM((n_time - 1, own_rows, CYL * NS), bf16),
+            dma((n_frames,)),
+            dma((quads,)),
+            dma((2,)),
+            dma((quads, n_feed)),
+            dma((quads, n_feed)),
+            dma((n_time - 1,)),
+            dma((n_time - 1,)),
+        ],
+        compiler_params=pltpu.CompilerParams(
+            collective_id=0, has_side_effects=True, vmem_limit_bytes=62 * 1024 * 1024
+        ),
+    )(voltages, coeffs, pfb_window(), feed_slot.reshape(n_feed, 1, inputs), t1, t2, upm)
+    return result.reshape(LIVE_DEV, UPCH, CYL * NS)
+
+
+def local(voltages, feed_slot, channel_flags):
+    fits = (
+        voltages.shape[0] == NS
+        and voltages.shape[1] == UPCH * 2 * CHANNELS
+        and lax.axis_size("tm") == 4
+        and lax.axis_size("feed") * voltages.shape[0] == 2 * CYL * NS
+    )
+    return (local_fused if fits else local_plain)(voltages, feed_slot, channel_flags)
+
+
 def solution(mesh):
     in_specs = (P("feed", "tm"), P(), P())
     out_specs = P(("feed", "tm"), None, None)

time: 156 us -> 84.5 us (0.54)
  Pallas kernels: 0 us -> 66.2 us
  matrix products: 56.5 us -> 0 us
  waiting for transfers between devices: 34.3 us -> 0 us
  local copies, waits for them, and re-layouts: 18.3 us -> 1.95 us
  blocking collectives: 10.9 us -> 0 us
  other arithmetic: 26.6 us -> 15.8 us
  starting transfers between devices: 9.17 us -> 0 us
    pallas_call x0 -> x1, Pallas kernels: none -> 66.2 us  [local_fused(): pl.pallas_call(functools.partial(fused_kernel, n_feed, n_time, n_frames,...]
    dot_general x4 -> x0, matrix products: 56.5 us -> none  [the longest x1 49.6 us: local(): jnp.einsum('rcs,ifs->rcfi', coeffs, filtered, preferred_element_type=jnp....]
    all_to_all x1 -> x0, waiting for transfers between devices: 34.3 us -> none  [local(): lax.all_to_all(spectra.reshape(2, n_feed, chans, n_frames, inputs), 'feed...]
    pad x1 -> x0, other arithmetic: 15.4 us -> none  [pfb_filter(): padded = jnp.pad(frames, ((0, 0), (TAPS - 1, TAPS - 1), (0, 0)))]
    all_to_all x1 -> x0, blocking collectives: 10.9 us -> none  [local(): lax.all_to_all(power.astype(jnp.bfloat16).reshape(n_time, LIVE_DEV, UPCH,...]
    convert_element_type x1 -> x0, local copies, waits for them, and re-layouts: 8.06 us -> none  [pfb_filter(): voltages.reshape(inputs, n_frames, 2 * CHANNELS).astype(jnp.float32)]
    convert_element_type x2 -> x1, other arithmetic: 0.12 us -> 7.63 us  [local_fused(): coeffs = coeffs.astype(bf16)]
    all_to_all x1 -> x0, starting transfers between devices: 6.75 us -> none  [local(): lax.all_to_all(spectra.reshape(2, n_feed, chans, n_frames, inputs), 'feed...]
  transfers between devices with their start and end apart: 2 -> 0, of which waited for: 1 -> 0; matrix products, arithmetic and copies ran while one was open for 2% -> 0% of each run, Pallas kernels for 0% -> 0%
where the time goes in v1:
time: 84.5 us; the launch traced here: 83.9 us
  Pallas kernels  66.2 us (78%)
  other arithmetic  15.8 us (19%)
  local copies, waits for them, and re-layouts  1.95 us (2%)
    pallas_call x1, Pallas kernels, local_fused(): pl.pallas_call(functools.partial(fused_kernel, n_feed, n_time, n_frames,...  66.2 us
    convert_element_type x1, other arithmetic, local_fused(): coeffs = coeffs.astype(bf16)  7.63 us

profile of v1, /device:TPU:0, one launch (start us, length us, event | category | flops | bytes accessed | tf_op | source)
XLA Modules:
  0.0 83.9 jit_solution(14080857877563983883)
XLA Ops:
  0.0 0.1 broadcast_in_dim.71
  0.1 0.7 iota_compare_fusion.2
  0.8 0.9 %select_reduce_fusion = s32[1024]{0:T(1024)S(1)} fusion(s32[1024]{0:T(1024)} %param.7), kind=kLoop, calls=%fused_computation | loop fusion | flops 3144704 | bytes 8192 | tf_op jit(solution)/shard_map/reduce_sum | solution.py:50
  1.7 0.1 convert_reduce_fusion
  1.8 0.1 reshape.102
  1.9 0.1 slice.6
  2.0 0.1 pad_add_fusion
  2.1 0.1 mul.198
  2.1 0.8 cosine_multiply_fusion
  2.9 0.8 sine_multiply_fusion
  3.7 0.9 %fusion.19.window = f32[4,2048]{1,0:T(4,128)} fusion(), kind=kLoop, calls=%fused_computation.44 | loop fusion | flops 344064 | bytes 32768 | tf_op jit(solution)/shard_map/mul | solution.py:31
  4.7 1.0 %fusion.13 = bf16[256,256]{1,0:T(8,128)(2,1)S(1)} fusion(), kind=kLoop, calls=%fused_computation.32 | loop fusion | flops 1245184 | bytes 131072 | tf_op jit(solution)/shard_map/neg | solution.py:392
  5.7 0.8 maximum_maximum_fusion.upm
  6.5 1.1 %multiply_convert_fusion.1 = (bf16[256,256]{1,0:T(8,128)(2,1)S(1)}, bf16[256,256]{1,0:T(8,128)(2,1)S(1)}) fusion(), kind=kLoop, calls=%fused_computation.25 | loop fusion | flops 1179648 | bytes 262144 | tf_op jit(solution)/shard_map/convert_element_type | solution.py:44
  7.6 0.8 pad_maximum_fusion.1
  8.5 7.6 %multiply_convert_fusion.coeffs = bf16[192,2048]{1,0:T(8,128)(2,1)} fusion(s32[192]{0:T(256)S(1)} %mul.198, pred[192]{0:T(512)(128)(4,1)S(1)} %broadcast_in_dim.71), kind=kLoop, calls=%fused_computation.8 | loop fusion | flops 7077888 | bytes 787392 | tf_op jit(solution)/shard_map/convert_element_type | solution.py:390
  16.1 66.2 %shard_map.55 = f32[48,1024]{1,0:T(8,128)} custom-call(bf16[256,32768]{1,0:T(8,128)(2,1)} %volt.1, bf16[192,2048]{1,0:T(8,128)(2,1)} %multiply_convert_fusion.coeffs, f32[4,2048]{1,0:T(4,128)} %fusion.19.window, s32[8,1,256]{2,1,0:T(1,128)} %bitcast.11, bf16[256,512]{1,0:T(8,128)(2,1)} %get-tuple-element.6.t1, bf16[256,512]{1,0:T(8,128)(2,1)} %get-tuple-element.5.t2, ...), custom_call_target="tpu_custom_call" | custom-call | tf_op jit(solution)/shard_map/pallas_call | solution.py:407
  82.3 1.6 %copy.7 = f32[3,16,1024]{2,1,0:T(8,128)} copy(f32[3,16,1024]{2,1,0:T(8,128)} %bitcast.6) | data formatting | bytes 393216
  (4 shorter events, 0.1 us)

commit v2 on v1

--- a/solution.py
+++ b/solution.py
@@ -4,6 +4,7 @@
 
 import jax
 import jax.numpy as jnp
+import numpy as np
 from jax import lax
 from jax.experimental import pallas as pl
 from jax.experimental.pallas import tpu as pltpu
@@ -124,8 +125,8 @@
 
 def fused_kernel(
     n_feed, n_time, n_frames, scale,
-    volt, coeffs, window, slots, t1, t2, upm, out,
-    vp, filt, tmp, send, recv, hist_out, hist_in, onehot, acc, cells, beams, power, psend, precv,
+    volt, trig, window, slots, t1, t2, upm, out,
+    vp, coeffs, filt, tmp, send, recv, hist_out, hist_in, onehot, acc, beams, power, psend, precv,
     load_sem, own_sem, hist_sem, send_sem, recv_sem, psend_sem, precv_sem,
 ):
     me = lax.axis_index("feed")
@@ -137,12 +138,17 @@
     rows = coeffs.shape[0]
     own_rows = LIVE_DEV * UPCH
 
+    def partner(m):
+        far = lax.rem(me // 4 + m // 4, 2)
+        near = lax.rem(lax.rem(me // 2, 2) + lax.rem(m // 2, 2), 2)
+        return far * 4 + near * 2 + lax.rem(lax.rem(me, 2) + lax.rem(m, 2), 2)
+
     def load(f):
         return pltpu.make_async_copy(
             volt.at[:, f * frame : (f + 1) * frame], vp.at[f + past], load_sem.at[f]
         )
 
-    order = list(range(n_frames - past, n_frames)) + list(range(1, n_frames - past)) + [0]
+    order = list(range(1, n_frames)) + [0]
     for f in order:
         load(f).start()
     barrier = pltpu.get_barrier_semaphore()
@@ -152,6 +158,11 @@
         pl.semaphore_signal(barrier, inc=1, device_id={"tm": lax.rem(tm + o, n_time)}, device_id_type=MESH)
     pl.semaphore_wait(barrier, n_feed - 1 + n_time - 1)
 
+    for k in range(frame // 128):
+        value = trig[:, 256 + k : 257 + k] * trig[:, :128]
+        value = value - trig[:, 256 + frame // 128 + k : 257 + frame // 128 + k] * trig[:, 128:256]
+        coeffs[:, k * 128 : (k + 1) * 128] = (value * (1.0 / math.sqrt(frame))).astype(jnp.bfloat16)
+
     for t in range(past):
         vp[t] = jnp.zeros_like(vp[t])
         vp[n_frames + past + t] = jnp.zeros_like(vp[t])
@@ -170,43 +181,30 @@
         lax.fori_loop(0, frame // width, chunk, 0)
         return lax.dot_general(coeffs[...], filt[...], NT, preferred_element_type=jnp.float32)
 
-    for f in range(n_frames - past, n_frames):
-        load(f).wait()
-
-    def tail_frame(k, _):
-        hist_out[k] = spectra(n_frames + k).astype(jnp.bfloat16)
-        return 0
-
-    lax.fori_loop(0, past, tail_frame, 0)
-
     def hist_copy(to):
         return pltpu.make_async_remote_copy(
             src_ref=hist_out, dst_ref=hist_in, send_sem=hist_sem.at[0], recv_sem=hist_sem.at[1],
             device_id={"tm": to}, device_id_type=MESH,
         )
 
-    @pl.when(tm < n_time - 1)
-    def _():
-        hist_copy(lax.rem(tm + 1, n_time)).start()
-
-    def send_copy(q, o):
-        to = lax.rem(me + o, n_feed)
+    def send_copy(q, m):
+        to = partner(m)
         return pltpu.make_async_remote_copy(
-            src_ref=send.at[q, to], dst_ref=recv.at[me, :, q],
-            send_sem=send_sem.at[q, o], recv_sem=recv_sem.at[q, o],
+            src_ref=send.at[q, to], dst_ref=recv.at[me, q],
+            send_sem=send_sem.at[q, m], recv_sem=recv_sem.at[q, m],
             device_id={"feed": to}, device_id_type=MESH,
         )
 
-    def arrival(q, o):
-        back = lax.rem(me + n_feed - o, n_feed)
+    def arrival(q, m):
+        back = partner(m)
         return pltpu.make_async_remote_copy(
-            src_ref=send.at[q, back], dst_ref=recv.at[back, :, q],
-            send_sem=send_sem.at[q, o], recv_sem=recv_sem.at[q, o],
+            src_ref=send.at[q, back], dst_ref=recv.at[back, q],
+            send_sem=send_sem.at[q, m], recv_sem=recv_sem.at[q, m],
             device_id={"feed": back}, device_id_type=MESH,
         )
 
     def own_copy(q):
-        return pltpu.make_async_copy(send.at[q, me], recv.at[me, :, q], own_sem.at[q])
+        return pltpu.make_async_copy(send.at[q, me], recv.at[me, q], own_sem.at[q])
 
     def far_first(k):
         return lax.rem(k + n_feed // 2 - 1, n_feed - 1) + 1
@@ -244,11 +242,25 @@
         lax.fori_loop(0, n_feed - 1, start, 0)
         own_copy(q).start()
 
-    for f in range(1, 4):
+    def tail_frames():
+        def tail_frame(k, _):
+            hist_out[k] = spectra(n_frames + k).astype(jnp.bfloat16)
+            return 0
+
+        lax.fori_loop(0, past, tail_frame, 0)
+
+        @pl.when(tm < n_time - 1)
+        def _():
+            hist_copy(lax.rem(tm + 1, n_time)).start()
+
+    for f in range(1, 8):
         load(f).wait()
-    for q in range(1, quads):
-        for f in range(4 * q, min(4 * q + 4, n_frames - past)):
+    quad(1, False)
+    for q in range(2, quads):
+        for f in range(4 * q, 4 * q + 4):
             load(f).wait()
+        if q == quads - 1:
+            tail_frames()
         quad(q, False)
     load(0).wait()
 
@@ -273,58 +285,69 @@
 
     step = 512
 
-    def place(s, fresh):
-        block = recv[s].reshape(2 * quads * 48, inputs)
+    def place(s, lo, hi, fresh):
+        count = hi - lo
+        block = recv[s, lo:hi].reshape(count * 96, inputs)
 
         def part(n, _):
             at = pl.multiple_of(n * step, step)
             got = lax.dot_general(block, onehot[s, pl.ds(at, step), :], NT, preferred_element_type=jnp.float32)
+            got = got.reshape(count, 2, 48, step)
             if fresh:
-                acc[:, pl.ds(at, step)] = got
+                acc[lo:hi, :, :, pl.ds(at, step)] = got
             else:
-                acc[:, pl.ds(at, step)] += got
+                acc[lo:hi, :, :, pl.ds(at, step)] += got
             return 0
 
         lax.fori_loop(0, total // step, part, 0)
 
-    for q in range(quads):
-        own_copy(q).wait()
-    place(me, True)
-
-    def source(k, _):
-        o = lax.rem(k, n_feed - 1) + 1
-        for q in range(quads):
-            arrival(q, o).wait_recv()
-        place(lax.rem(me + n_feed - o, n_feed), False)
-        return 0
-
-    lax.fori_loop(0, n_feed - 1, source, 0)
-    half = quads * 48
-    cells[...] = acc[...].astype(jnp.bfloat16)
-
-    for p in range(2):
-        z = []
-        for y in range(CYL):
-            at = (p * CYL + y) * NS
-            value = jnp.dot(cells[:half, at : at + NS], t1[...], preferred_element_type=jnp.float32)
-            value = value + jnp.dot(cells[half:, at : at + NS], t2[...], preferred_element_type=jnp.float32)
-            z.append((value[:, :NS], value[:, NS:]))
-        (r0, i0), (r1, i1), (r2, i2), (r3, i3) = z
-        t0r, t1r, t2r, t3r = r0 + r2, r0 - r2, r1 + r3, r1 - r3
-        t0i, t1i, t2i, t3i = i0 + i2, i0 - i2, i1 + i3, i1 - i3
-        re = [t0r + t2r, t1r + t3i, t0r - t2r, t1r - t3i]
-        im = [t0i + t2i, t1i - t3r, t0i - t2i, t1i + t3r]
-        for e in range(CYL):
-            at = (p * CYL + e) * NS
-            beams[:half, at : at + NS] = (re[e] * 0.5).astype(jnp.bfloat16)
-            beams[half:, at : at + NS] = (im[e] * 0.5).astype(jnp.bfloat16)
+    def gather(lo, hi):
+        for q in range(lo, hi):
+            own_copy(q).wait()
+        place(me, lo, hi, True)
+
+        def source(k, _):
+            for q in range(lo, hi):
+                arrival(q, k + 1).wait_recv()
+            place(partner(k + 1), lo, hi, False)
+            return 0
+
+        lax.fori_loop(0, n_feed - 1, source, 0)
+
+    def beamform(lo, hi):
+        count = hi - lo
+
+        def cells(part, at):
+            return acc[lo:hi, part, :, at : at + NS].reshape(count * 48, NS).astype(jnp.bfloat16)
+
+        for p in range(2):
+            z = []
+            for y in range(CYL):
+                at = (p * CYL + y) * NS
+                value = jnp.dot(cells(0, at), t1[...], preferred_element_type=jnp.float32)
+                value = value + jnp.dot(cells(1, at), t2[...], preferred_element_type=jnp.float32)
+                z.append((value[:, :NS], value[:, NS:]))
+            (r0, i0), (r1, i1), (r2, i2), (r3, i3) = z
+            t0r, t1r, t2r, t3r = r0 + r2, r0 - r2, r1 + r3, r1 - r3
+            t0i, t1i, t2i, t3i = i0 + i2, i0 - i2, i1 + i3, i1 - i3
+            re = [t0r + t2r, t1r + t3i, t0r - t2r, t1r - t3i]
+            im = [t0i + t2i, t1i - t3r, t0i - t2i, t1i + t3r]
+            for e in range(CYL):
+                at = (p * CYL + e) * NS
+                for part, value in ((0, re[e]), (1, im[e])):
+                    beams[part, lo:hi, :, at : at + NS] = (value * 0.5).astype(jnp.bfloat16).reshape(count, 48, NS)
+
+    gather(1, quads)
+    beamform(1, quads)
+    gather(0, 1)
+    beamform(0, 1)
 
     outs = upm.shape[0] // 2
     for e in range(CYL):
         summed = 0.0
         for p in range(2):
             at = (p * CYL + e) * NS
-            up = jnp.dot(upm[...], beams[:, at : at + NS], preferred_element_type=jnp.float32)
+            up = jnp.dot(upm[...], beams[:, :, :, at : at + NS].reshape(-1, NS), preferred_element_type=jnp.float32)
             summed = summed + up[:outs] * up[:outs] + up[outs:] * up[outs:]
         summed = summed * scale
         for t in range(n_time):
@@ -369,7 +392,25 @@
             f = 4 * q + 2 * pair
             frames += [f] * 8 + [f + 1] * 8 + [f] * 4 + [f + 1] * 4
             chans += list(range(8)) * 2 + list(range(8, 12)) * 2
-    return jnp.array(frames, jnp.int32), jnp.array(chans, jnp.int32)
+    return np.array(frames), np.array(chans)
+
+
+def rounded_pair(modulus, first, second):
+    angle = (first[:, None] * second[None, :] % modulus) * (2.0 * np.pi / modulus)
+    scale = 1.0 / np.sqrt(modulus)
+    bf16 = jnp.bfloat16
+    return (
+        (np.cos(angle) * scale).astype(np.float32).astype(bf16),
+        (np.sin(angle) * scale).astype(np.float32).astype(bf16),
+    )
+
+
+def window_table():
+    length = TAPS * 2 * CHANNELS
+    sample = np.arange(length)
+    offset = (sample - length / 2 + 0.5) / (2 * CHANNELS)
+    taper = 0.5 - 0.5 * np.cos(2.0 * np.pi * (sample + 0.5) / length)
+    return (np.sinc(offset) * taper).astype(np.float32).reshape(TAPS, 2 * CHANNELS)
 
 
 def local_fused(voltages, feed_slot, channel_flags):
@@ -383,25 +424,30 @@
     quads = n_frames // 4
     live = live_channels(channel_flags, chans * n_feed).reshape(n_feed, chans)
     row_chan = jnp.concatenate([live, live[:, 8:], live[:, :8]], axis=1).reshape(-1)
-    is_imag = jnp.tile(jnp.arange(2 * chans) >= chans, n_feed)
-    product = row_chan[:, None] * jnp.arange(frame, dtype=jnp.int32)[None, :] % frame
-    angle = product.astype(jnp.float32) * (2.0 * jnp.pi / frame)
-    coeffs = jnp.where(is_imag[:, None], -jnp.sin(angle), jnp.cos(angle)) * (1.0 / math.sqrt(frame))
-    coeffs = coeffs.astype(bf16)
-    c, d = grid_table()
-    t1 = jnp.concatenate([c, -d], axis=1)
-    t2 = jnp.concatenate([d, c], axis=1)
-    index = jnp.arange(UPCH, dtype=jnp.int32)
+    quarter = frame // 4
+    shift = np.tile(np.where(np.arange(2 * chans) >= chans, quarter, 0), n_feed)
+    fine = np.arange(128)
+    coarse = np.arange(frame // 128) * 128
+    step = jnp.array(np.concatenate([fine, fine, coarse, coarse]), jnp.int32)
+    lag = np.concatenate([fine * 0, fine * 0 + quarter, coarse * 0, coarse * 0 + quarter])
+    turned = np.concatenate([fine * 0, fine * 0, coarse * 0 + 1, coarse * 0 + 1])
+    extra = jnp.array(shift[:, None] * turned[None, :] + frame - lag[None, :], jnp.int32)
+    product = (row_chan[:, None] * step[None, :] + extra) % frame
+    trig = jnp.cos(product.astype(jnp.float32) * (2.0 * jnp.pi / frame))
+    index = np.arange(NS)
+    c, d = rounded_pair(NS, index, index)
+    t1 = jnp.array(np.concatenate([c, -d], axis=1))
+    t2 = jnp.array(np.concatenate([d, c], axis=1))
     frames, row_ch = row_order(quads)
-    up_cos, up_sin = phase_pair(UPCH, index, frames, 1.0 / math.sqrt(UPCH))
-    same = (jnp.arange(chans)[:, None] == row_ch[None, :])[:, None, :]
-    cm = jnp.where(same, up_cos[None], 0.0).reshape(chans * UPCH, -1)
-    sm = jnp.where(same, up_sin[None], 0.0).reshape(chans * UPCH, -1)
-    upm = jnp.concatenate([jnp.concatenate([cm, sm], 1), jnp.concatenate([-sm, cm], 1)], 0).astype(bf16)
+    up_cos, up_sin = rounded_pair(UPCH, np.arange(UPCH), frames)
+    same = (np.arange(chans)[:, None] == row_ch[None, :])[:, None, :].astype(np.float32)
+    cm = (same * up_cos.astype(np.float32)[None]).reshape(chans * UPCH, -1)
+    sm = (same * up_sin.astype(np.float32)[None]).reshape(chans * UPCH, -1)
+    upm = np.concatenate([np.concatenate([cm, sm], 1), np.concatenate([-sm, cm], 1)], 0)
+    upm = jnp.array(upm.astype(bf16))
     rows = 2 * chans * n_feed
     total = n_feed * inputs
     own_rows = LIVE_DEV * UPCH
-    half = quads * 48
     vmem = pl.BlockSpec(memory_space=pltpu.VMEM)
     dma = pltpu.SemaphoreType.DMA
     result = pl.pallas_call(
@@ -411,16 +457,16 @@
         out_specs=vmem,
         scratch_shapes=[
             pltpu.VMEM((n_frames + 2 * TAPS - 2, inputs, frame), bf16),
+            pltpu.VMEM((rows, frame), bf16),
             pltpu.VMEM((inputs, frame), bf16),
             pltpu.VMEM((4, rows, inputs), jnp.float32),
             pltpu.VMEM((quads, n_feed, 2, 48, inputs), bf16),
-            pltpu.VMEM((n_feed, 2, quads, 48, inputs), bf16),
+            pltpu.VMEM((n_feed, quads, 2, 48, inputs), bf16),
             pltpu.VMEM((TAPS - 1, rows, inputs), bf16),
             pltpu.VMEM((TAPS - 1, rows, inputs), bf16),
             pltpu.VMEM((n_feed, total, inputs), bf16),
-            pltpu.VMEM((2 * half, total), jnp.float32),
-            pltpu.VMEM((2 * half, total), bf16),
-            pltpu.VMEM((2 * half, total), bf16),
+            pltpu.VMEM((quads, 2, 48, total), jnp.float32),
+            pltpu.VMEM((2, quads, 48, total), bf16),
             pltpu.VMEM((n_time, own_rows, CYL * NS), jnp.float32),
             pltpu.VMEM((n_time, own_rows, CYL * NS), bf16),
             pltpu.VMEM((n_time - 1, own_rows, CYL * NS), bf16),
@@ -435,7 +481,7 @@
         compiler_params=pltpu.CompilerParams(
             collective_id=0, has_side_effects=True, vmem_limit_bytes=62 * 1024 * 1024
         ),
-    )(voltages, coeffs, pfb_window(), feed_slot.reshape(n_feed, 1, inputs), t1, t2, upm)
+    )(voltages, trig, jnp.array(window_table()), feed_slot.reshape(n_feed, 1, inputs), t1, t2, upm)
     return result.reshape(LIVE_DEV, UPCH, CYL * NS)
 
 
@@ -444,6 +490,7 @@
         voltages.shape[0] == NS
         and voltages.shape[1] == UPCH * 2 * CHANNELS
         and lax.axis_size("tm") == 4
+        and lax.axis_size("feed") == 8
         and lax.axis_size("feed") * voltages.shape[0] == 2 * CYL * NS
     )
     return (local_fused if fits else local_plain)(voltages, feed_slot, channel_flags)

time: 84.5 us -> 69.7 us (0.82)
  other arithmetic: 15.8 us -> 3.95 us
  Pallas kernels: 66.2 us -> 63.3 us
    convert_element_type x2 -> x0, other arithmetic: 8.74 us -> none  [the longest x1 7.63 us: local_fused(): coeffs = coeffs.astype(bf16)]
    pallas_call x1, Pallas kernels: 66.2 us -> 63.3 us  [local_fused(): pl.pallas_call(functools.partial(fused_kernel, n_feed, n_time, n_frames,...]
    cos x0 -> x1, other arithmetic: none -> 2.84 us  [local_fused(): trig = jnp.cos(product.astype(jnp.float32) * (2.0 * jnp.pi / frame))]
    mul x3 -> x0, other arithmetic: 2.49 us -> none  [the longest x2 1.54 us: phase_pair(): return (jnp.cos(angle) * scale, jnp.sin(angle) * scale)]
    concatenate x2 -> x0, other arithmetic: 1.67 us -> none  [the longest x1 0.84 us: local_fused(): jnp.concatenate([jnp.concatenate([cm, sm], 1), jnp.concatenate([-sm, cm],...]
    neg x1 -> x0, other arithmetic: 0.99 us -> none  [local_fused(): t1 = jnp.concatenate([c, -d], axis=1)]
where the time goes in v2:
time: 69.7 us; the launch traced here: 69.1 us
  Pallas kernels  63.3 us (91%)
  other arithmetic  3.95 us (6%)
  local copies, waits for them, and re-layouts  1.85 us (3%)
    pallas_call x1, Pallas kernels, local_fused(): pl.pallas_call(functools.partial(fused_kernel, n_feed, n_time, n_frames,...  63.3 us
    cos x1, other arithmetic, local_fused(): trig = jnp.cos(product.astype(jnp.float32) * (2.0 * jnp.pi / frame))  2.84 us
    unnamed x1, local copies, waits for them, and re-layouts  1.62 us

profile of v2, /device:TPU:0, one launch (start us, length us, event | category | flops | bytes accessed | tf_op | source)
XLA Modules:
  0.0 69.1 jit_solution(8400499227275171000)
XLA Ops:
  0.0 0.9 %select_reduce_fusion = s32[1024]{0:T(1024)S(1)} fusion(s32[1024]{0:T(1024)} %param.11), kind=kLoop, calls=%fused_computation | loop fusion | flops 3144704 | bytes 8192 | tf_op jit(solution)/shard_map/reduce_sum | solution.py:51
  0.9 0.1 convert_reduce_fusion
  1.0 0.1 reshape.13
  1.1 0.1 slice.6
  1.2 0.1 pad_add_fusion
  1.3 0.1 mul.21
  1.3 2.8 %fusion.3.trig = f32[192,288]{1,0:T(8,128)} fusion(s32[192,288]{1,0:T(8,128)} %constant.31.clone, s32[288]{0:T(512)} %constant.30.clone, s32[192]{0:T(256)S(1)} %mul.21), kind=kLoop, calls=%fused_computation.10 | loop fusion | flops 829440 | bytes 444288 | tf_op jit(solution)/shard_map/cos | solution.py:436
  4.2 63.3 %shard_map.91 = f32[48,1024]{1,0:T(8,128)} custom-call(bf16[256,32768]{1,0:T(8,128)(2,1)} %volt.1, f32[192,288]{1,0:T(8,128)} %fusion.3.trig, f32[4,2048]{1,0:T(4,128)} %constant.35.clone.window, s32[8,1,256]{2,1,0:T(1,128)} %bitcast.5, bf16[256,512]{1,0:T(8,128)(2,1)} %constant.32.clone.t1, bf16[256,512]{1,0:T(8,128)(2,1)} %constant.33.clone.t2, ...), custom_call_target="tpu_custom_call" | custom-call | tf_op jit(solution)/shard_map/pallas_call | solution.py:453
  67.5 1.6 %copy.11 = f32[3,16,1024]{2,1,0:T(8,128)} copy(f32[3,16,1024]{2,1,0:T(8,128)} %bitcast.3) | data formatting | bytes 393216

commit v3 on v2

--- a/solution.py
+++ b/solution.py
@@ -320,13 +320,14 @@
         def cells(part, at):
             return acc[lo:hi, part, :, at : at + NS].reshape(count * 48, NS).astype(jnp.bfloat16)
 
+        stacked = [jnp.concatenate([cells(part, g * NS) for g in range(2 * CYL)], axis=0) for part in range(2)]
+        value = jnp.dot(stacked[0], t1[...], preferred_element_type=jnp.float32)
+        value = value + jnp.dot(stacked[1], t2[...], preferred_element_type=jnp.float32)
         for p in range(2):
             z = []
             for y in range(CYL):
-                at = (p * CYL + y) * NS
-                value = jnp.dot(cells(0, at), t1[...], preferred_element_type=jnp.float32)
-                value = value + jnp.dot(cells(1, at), t2[...], preferred_element_type=jnp.float32)
-                z.append((value[:, :NS], value[:, NS:]))
+                one = value[(p * CYL + y) * count * 48 : (p * CYL + y + 1) * count * 48]
+                z.append((one[:, :NS], one[:, NS:]))
             (r0, i0), (r1, i1), (r2, i2), (r3, i3) = z
             t0r, t1r, t2r, t3r = r0 + r2, r0 - r2, r1 + r3, r1 - r3
             t0i, t1i, t2i, t3i = i0 + i2, i0 - i2, i1 + i3, i1 - i3
@@ -334,13 +335,21 @@
             im = [t0i + t2i, t1i - t3r, t0i - t2i, t1i + t3r]
             for e in range(CYL):
                 at = (p * CYL + e) * NS
-                for part, value in ((0, re[e]), (1, im[e])):
-                    beams[part, lo:hi, :, at : at + NS] = (value * 0.5).astype(jnp.bfloat16).reshape(count, 48, NS)
+                for part, beam in ((0, re[e]), (1, im[e])):
+                    beams[part, lo:hi, :, at : at + NS] = (beam * 0.5).astype(jnp.bfloat16).reshape(count, 48, NS)
 
     gather(1, quads)
     beamform(1, quads)
     gather(0, 1)
     beamform(0, 1)
+
+    def power_copy(o, e):
+        to = lax.rem(tm + o, n_time)
+        return pltpu.make_async_remote_copy(
+            src_ref=psend.at[e, to], dst_ref=precv.at[o - 1, e],
+            send_sem=psend_sem.at[o - 1, e], recv_sem=precv_sem.at[o - 1, e],
+            device_id={"tm": to}, device_id_type=MESH,
+        )
 
     outs = upm.shape[0] // 2
     for e in range(CYL):
@@ -349,29 +358,20 @@
             at = (p * CYL + e) * NS
             up = jnp.dot(upm[...], beams[:, :, :, at : at + NS].reshape(-1, NS), preferred_element_type=jnp.float32)
             summed = summed + up[:outs] * up[:outs] + up[outs:] * up[outs:]
-        summed = summed * scale
-        for t in range(n_time):
-            block = summed[t * own_rows : (t + 1) * own_rows]
-            power[t, :, e * NS : (e + 1) * NS] = block
-            psend[t, :, e * NS : (e + 1) * NS] = block.astype(jnp.bfloat16)
-
-    def power_copy(o):
-        to = lax.rem(tm + o, n_time)
-        return pltpu.make_async_remote_copy(
-            src_ref=psend.at[to], dst_ref=precv.at[o - 1],
-            send_sem=psend_sem.at[o - 1], recv_sem=precv_sem.at[o - 1],
-            device_id={"tm": to}, device_id_type=MESH,
-        )
-
-    for o in range(1, n_time):
-        power_copy(o).start()
-    result = power[tm]
-    for o in range(1, n_time):
-        power_copy(o).wait_recv()
-        result = result + precv[o - 1].astype(jnp.float32)
-    out[...] = result
-    for o in range(1, n_time):
-        power_copy(o).wait_send()
+        summed = (summed * scale).reshape(n_time, own_rows, NS)
+        power[e] = summed
+        psend[e] = summed.astype(jnp.bfloat16)
+        for o in range(1, n_time):
+            power_copy(o, e).start()
+    for e in range(CYL):
+        result = power[e, tm]
+        for o in range(1, n_time):
+            power_copy(o, e).wait_recv()
+            result = result + precv[o - 1, e].astype(jnp.float32)
+        out[:, e * NS : (e + 1) * NS] = result
+    for e in range(CYL):
+        for o in range(1, n_time):
+            power_copy(o, e).wait_send()
 
     def drain(k, _):
         for q in range(quads):
@@ -432,7 +432,7 @@
     lag = np.concatenate([fine * 0, fine * 0 + quarter, coarse * 0, coarse * 0 + quarter])
     turned = np.concatenate([fine * 0, fine * 0, coarse * 0 + 1, coarse * 0 + 1])
     extra = jnp.array(shift[:, None] * turned[None, :] + frame - lag[None, :], jnp.int32)
-    product = (row_chan[:, None] * step[None, :] + extra) % frame
+    product = (row_chan[:, None] * step[None, :] + extra) & (frame - 1)
     trig = jnp.cos(product.astype(jnp.float32) * (2.0 * jnp.pi / frame))
     index = np.arange(NS)
     c, d = rounded_pair(NS, index, index)
@@ -467,16 +467,16 @@
             pltpu.VMEM((n_feed, total, inputs), bf16),
             pltpu.VMEM((quads, 2, 48, total), jnp.float32),
             pltpu.VMEM((2, quads, 48, total), bf16),
-            pltpu.VMEM((n_time, own_rows, CYL * NS), jnp.float32),
-            pltpu.VMEM((n_time, own_rows, CYL * NS), bf16),
-            pltpu.VMEM((n_time - 1, own_rows, CYL * NS), bf16),
+            pltpu.VMEM((CYL, n_time, own_rows, NS), jnp.float32),
+            pltpu.VMEM((CYL, n_time, own_rows, NS), bf16),
+            pltpu.VMEM((n_time - 1, CYL, own_rows, NS), bf16),
             dma((n_frames,)),
             dma((quads,)),
             dma((2,)),
             dma((quads, n_feed)),
             dma((quads, n_feed)),
-            dma((n_time - 1,)),
-            dma((n_time - 1,)),
+            dma((n_time - 1, CYL)),
+            dma((n_time - 1, CYL)),
         ],
         compiler_params=pltpu.CompilerParams(
             collective_id=0, has_side_effects=True, vmem_limit_bytes=62 * 1024 * 1024

time: 69.7 us -> 69.1 us (level)
  no operation moved by 1% of the time
where the time goes in v3:
time: 69.1 us; the launch traced here: 68.8 us
  Pallas kernels  63.1 us (91%)
  other arithmetic  3.85 us (6%)
  local copies, waits for them, and re-layouts  1.85 us (3%)
    pallas_call x1, Pallas kernels, local_fused(): pl.pallas_call(functools.partial(fused_kernel, n_feed, n_time, n_frames,...  63.1 us
    cos x1, other arithmetic, local_fused(): trig = jnp.cos(product.astype(jnp.float32) * (2.0 * jnp.pi / frame))  2.75 us
    unnamed x1, local copies, waits for them, and re-layouts  1.62 us

profile of v3, /device:TPU:0, one launch (start us, length us, event | category | flops | bytes accessed | tf_op | source)
XLA Modules:
  0.0 68.8 jit_solution(17577337364472962370)
XLA Ops:
  0.0 0.9 %select_reduce_fusion = s32[1024]{0:T(1024)S(1)} fusion(s32[1024]{0:T(1024)} %param.11), kind=kLoop, calls=%fused_computation | loop fusion | flops 3144704 | bytes 8192 | tf_op jit(solution)/shard_map/reduce_sum | solution.py:51
  0.9 0.1 convert_reduce_fusion
  1.0 0.1 reshape.13
  1.1 0.1 slice.6
  1.2 0.1 pad_add_fusion
  1.3 0.1 mul.21
  1.3 2.7 %multiply_cosine_fusion.trig = f32[192,288]{1,0:T(8,128)} fusion(s32[192,288]{1,0:T(8,128)} %constant.19.clone, s32[288]{0:T(512)} %constant.18.clone, s32[192]{0:T(256)S(1)} %mul.21), kind=kLoop, calls=%fused_computation.4 | loop fusion | flops 276480 | bytes 444288 | tf_op jit(solution)/shard_map/cos | solution.py:436
  4.1 63.1 %shard_map.91 = f32[48,1024]{1,0:T(8,128)} custom-call(bf16[256,32768]{1,0:T(8,128)(2,1)} %volt.1, f32[192,288]{1,0:T(8,128)} %multiply_cosine_fusion.trig, f32[4,2048]{1,0:T(4,128)} %constant.23.clone.window, s32[8,1,256]{2,1,0:T(1,128)} %bitcast.5, bf16[256,512]{1,0:T(8,128)(2,1)} %constant.20.clone.t1, bf16[256,512]{1,0:T(8,128)(2,1)} %constant.21.clone.t2, ...), custom_call_target="tpu_custom_call" | custom-call | tf_op jit(solution)/shard_map/pallas_call | solution.py:453
  67.2 1.6 %copy.11 = f32[3,16,1024]{2,1,0:T(8,128)} copy(f32[3,16,1024]{2,1,0:T(8,128)} %bitcast.3) | data formatting | bytes 393216

commit v4 on v3

--- a/solution.py
+++ b/solution.py
@@ -156,16 +156,11 @@
         pl.semaphore_signal(barrier, inc=1, device_id={"feed": lax.rem(me + o, n_feed)}, device_id_type=MESH)
     for o in range(1, n_time):
         pl.semaphore_signal(barrier, inc=1, device_id={"tm": lax.rem(tm + o, n_time)}, device_id_type=MESH)
-    pl.semaphore_wait(barrier, n_feed - 1 + n_time - 1)
 
     for k in range(frame // 128):
         value = trig[:, 256 + k : 257 + k] * trig[:, :128]
         value = value - trig[:, 256 + frame // 128 + k : 257 + frame // 128 + k] * trig[:, 128:256]
         coeffs[:, k * 128 : (k + 1) * 128] = (value * (1.0 / math.sqrt(frame))).astype(jnp.bfloat16)
-
-    for t in range(past):
-        vp[t] = jnp.zeros_like(vp[t])
-        vp[n_frames + past + t] = jnp.zeros_like(vp[t])
 
     def spectra(f):
         width = 256
@@ -235,6 +230,9 @@
 
         lax.fori_loop(0, n_feed, pack, 0)
 
+        if q == 1:
+            pl.semaphore_wait(barrier, n_feed - 1 + n_time - 1)
+
         def start(k, _):
             send_copy(q, far_first(k)).start()
             return 0
@@ -256,6 +254,9 @@
     for f in range(1, 8):
         load(f).wait()
     quad(1, False)
+    for t in range(past):
+        vp[t] = jnp.zeros_like(vp[t])
+        vp[n_frames + past + t] = jnp.zeros_like(vp[t])
     for q in range(2, quads):
         for f in range(4 * q, 4 * q + 4):
             load(f).wait()

time: 69.1 us -> 68.6 us (level)
  no operation moved by 1% of the time
where the time goes in v4:
time: 68.6 us; the launch traced here: 68.4 us
  Pallas kernels  62.6 us (91%)
  other arithmetic  3.85 us (6%)
  local copies, waits for them, and re-layouts  1.85 us (3%)
    pallas_call x1, Pallas kernels, local_fused(): pl.pallas_call(functools.partial(fused_kernel, n_feed, n_time, n_frames,...  62.6 us
    cos x1, other arithmetic, local_fused(): trig = jnp.cos(product.astype(jnp.float32) * (2.0 * jnp.pi / frame))  2.75 us
    unnamed x1, local copies, waits for them, and re-layouts  1.62 us

profile of v4, /device:TPU:0, one launch (start us, length us, event | category | flops | bytes accessed | tf_op | source)
XLA Modules:
  0.0 68.4 jit_solution(12433542785398397555)
XLA Ops:
  0.0 0.9 %select_reduce_fusion = s32[1024]{0:T(1024)S(1)} fusion(s32[1024]{0:T(1024)} %param.11), kind=kLoop, calls=%fused_computation | loop fusion | flops 3144704 | bytes 8192 | tf_op jit(solution)/shard_map/reduce_sum | solution.py:51
  0.9 0.1 convert_reduce_fusion
  1.0 0.1 reshape.13
  1.1 0.1 slice.6
  1.2 0.1 pad_add_fusion
  1.3 0.1 mul.21
  1.3 2.7 %multiply_cosine_fusion.trig = f32[192,288]{1,0:T(8,128)} fusion(s32[192,288]{1,0:T(8,128)} %constant.19.clone, s32[288]{0:T(512)} %constant.18.clone, s32[192]{0:T(256)S(1)} %mul.21), kind=kLoop, calls=%fused_computation.4 | loop fusion | flops 276480 | bytes 444288 | tf_op jit(solution)/shard_map/cos | solution.py:437
  4.1 62.6 %shard_map.91 = f32[48,1024]{1,0:T(8,128)} custom-call(bf16[256,32768]{1,0:T(8,128)(2,1)} %volt.1, f32[192,288]{1,0:T(8,128)} %multiply_cosine_fusion.trig, f32[4,2048]{1,0:T(4,128)} %constant.23.clone.window, s32[8,1,256]{2,1,0:T(1,128)} %bitcast.5, bf16[256,512]{1,0:T(8,128)(2,1)} %constant.20.clone.t1, bf16[256,512]{1,0:T(8,128)(2,1)} %constant.21.clone.t2, ...), custom_call_target="tpu_custom_call" | custom-call | tf_op jit(solution)/shard_map/pallas_call | solution.py:454
  66.7 1.6 %copy.11 = f32[3,16,1024]{2,1,0:T(8,128)} copy(f32[3,16,1024]{2,1,0:T(8,128)} %bitcast.3) | data formatting | bytes 393216
